TPU v7x, 256 devices: a whole 4x4x8 slice. The times are simulated.
256 devices in a mesh: group: 16 (over z_lo, y), tok: 16 (over z_hi, x, core).
Axes of the slice: x: 4, y: 4, z: 8 (z_hi: 2, z_lo: 4; z = z_hi * 4 + z_lo), core: 2. Of those that a mesh axis runs over, the one named last changes fastest.
Arguments:
- tokens: bfloat16 [131072, 2048], P(('group', 'tok')), may hold values from -94 to 94
- learning_rates: float32 [2, 131072], P(None, 'group'), may hold values from 0.1 to 1
- channel_gains: float32 [2, 5, 2048], P(None, None, 'tok'), may hold values from 0.3 to 3
- fast_init: float32 [2, 3, 16, 128, 128], P(None, None, 'tok'), may hold values from -0.5 to 0.5
- step_size: float32 [2, 16], P(None, 'tok'), may hold values from 0.05 to 1
- update_table: int32 [2, 16], replicated, may hold values 0 or 1
Outputs:
- mixed: bfloat16 [131072, 2048], P(('group', 'tok'))
All inputs are finite; a program needn't handle non-finite values.
Results may differ from a plain program's by a relative error of at most 0.033.
Values may be sent and summed in bfloat16 or wider, within the bound.
No kernel may reach another device: no remote copies, remote signals or barrier semaphores. Data moves between devices by JAX's collectives and lax.ppermute only.
A program may use at most 64 MiB of HBM per device.

v0:
```python
import jax
import jax.numpy as jnp
from jax import lax
from jax.sharding import PartitionSpec as P

NS_STEPS = 5
MUON_A = 3.4445
MUON_B = -4.775
MUON_C = 2.0315
EPSILON = 1e-06


def passed_along(value, axis, by):
    size = lax.axis_size(axis)
    pairs = [(i, i + by) for i in range(size) if 0 <= i + by < size]
    return lax.ppermute(value, axis, pairs)


def orthogonalize(gradient):
    scaling = lax.rsqrt(jnp.sum(gradient * gradient, axis=(-2, -1), keepdims=True) + EPSILON)
    current = gradient * scaling
    for repeat in range(NS_STEPS):
        square = jnp.einsum("...ij,...kj->...ik", current, current, precision=lax.Precision.HIGHEST)
        polynom = MUON_B * square + MUON_C * jnp.einsum(
            "...ij,...jk->...ik", square, square, precision=lax.Precision.HIGHEST
        )
        current = MUON_A * current + jnp.einsum(
            "...ij,...jk->...ik", polynom, current, precision=lax.Precision.HIGHEST
        )
    return current


def layer_group(stream, entering, gain_rows, rates_row, steps_row, update_flag, inverse):
    row_count, channel_count = stream.shape
    heads_n = entering.shape[1]
    head_dim = entering.shape[2]
    normed = stream.astype(jnp.float32) * inverse[:, None] * gain_rows[0]
    queries = (normed * gain_rows[1]).astype(jnp.bfloat16).reshape(row_count, heads_n, head_dim)
    keys_in = (normed * gain_rows[2]).astype(jnp.bfloat16).reshape(row_count, heads_n, head_dim)
    values_in = (normed * gain_rows[3]).astype(jnp.bfloat16).reshape(row_count, heads_n, head_dim)
    rounded = entering.astype(jnp.bfloat16)
    gate_q = jnp.einsum("thi,hij->thj", queries, rounded[0], preferred_element_type=jnp.float32)
    up_q = jnp.einsum("thi,hij->thj", queries, rounded[1], preferred_element_type=jnp.float32)
    hidden_q = (jax.nn.silu(gate_q) * up_q).astype(jnp.bfloat16)
    output = jnp.einsum(
        "thj,hjk->thk", hidden_q, rounded[2], preferred_element_type=jnp.float32
    ).reshape(row_count, channel_count)
    mixed_rows = (stream.astype(jnp.float32) + gain_rows[4] * output).astype(jnp.bfloat16)
    gate_k = jnp.einsum("thi,hij->thj", keys_in, rounded[0], preferred_element_type=jnp.float32)
    up_k = jnp.einsum("thi,hij->thj", keys_in, rounded[1], preferred_element_type=jnp.float32)
    sigmoid_k = jax.nn.sigmoid(gate_k)
    active_k = gate_k * sigmoid_k
    hidden_k = (active_k * up_k).astype(jnp.bfloat16)
    targets = (rates_row[:, None, None] * values_in.astype(jnp.float32)).astype(jnp.bfloat16)
    back_hidden = jnp.einsum(
        "thk,hjk->thj", targets, rounded[2], preferred_element_type=jnp.float32
    )
    back_up = (back_hidden * active_k).astype(jnp.bfloat16)
    back_gate = (back_hidden * up_k * sigmoid_k * (1.0 + gate_k * (1.0 - sigmoid_k))).astype(
        jnp.bfloat16
    )
    grad_gate = jnp.einsum("thi,thj->hij", keys_in, back_gate, preferred_element_type=jnp.float32)
    grad_up = jnp.einsum("thi,thj->hij", keys_in, back_up, preferred_element_type=jnp.float32)
    grad_down = jnp.einsum("thj,thk->hjk", hidden_k, targets, preferred_element_type=jnp.float32)
    direction = orthogonalize(jnp.stack([grad_gate, grad_up, grad_down]))
    moved_state = entering + (update_flag * steps_row)[None, :, None, None] * direction
    norm_before = jnp.sqrt(jnp.sum(entering * entering, axis=2, keepdims=True) + EPSILON)
    norm_after = jnp.sqrt(jnp.sum(moved_state * moved_state, axis=2, keepdims=True) + EPSILON)
    return (mixed_rows, moved_state * (norm_before / norm_after))


def pass_on(outgoing):
    return passed_along(outgoing, "group", 1)


def body(tokens, learning_rates, channel_gains, fast_init, step_size, update_table):
    start_stream = lax.all_to_all(tokens, "tok", split_axis=1, concat_axis=0, tiled=True)
    group_count = lax.axis_size("group")
    group_index = lax.axis_index("group")
    width_all = start_stream.shape[1] * lax.axis_size("tok")
    layer_count = fast_init.shape[0]
    zero_state = jnp.zeros(fast_init.shape[1:], jnp.float32)

    def tick_work(stream, outgoing, layer_now, active, inverse):
        received = pass_on(outgoing)
        initial = lax.dynamic_index_in_dim(fast_init, layer_now, 0, keepdims=False)
        entering = jnp.where(group_index == 0, initial, received)
        gain_rows = lax.dynamic_index_in_dim(channel_gains, layer_now, 0, keepdims=False)
        rates_row = lax.dynamic_index_in_dim(learning_rates, layer_now, 0, keepdims=False)
        steps_row = lax.dynamic_index_in_dim(step_size, layer_now, 0, keepdims=False)
        table_cell = lax.dynamic_slice(
            update_table, (jnp.asarray(layer_now, jnp.int32), group_index), (1, 1)
        )
        update_flag = table_cell[0, 0].astype(jnp.float32)

        def working(operands):
            return layer_group(
                operands[0], operands[1], gain_rows, rates_row, steps_row, update_flag, inverse
            )

        def resting(operands):
            return (operands[0], operands[2])

        return lax.cond(active, working, resting, (stream, entering, outgoing))

    final_stream = start_stream
    for layer_now in range(layer_count):
        widened = final_stream.astype(jnp.float32)
        totals = lax.psum(jnp.sum(widened * widened, axis=1), "tok")
        inverse = lax.rsqrt(totals / width_all + EPSILON)

        def one_tick(tick_index, loop_state):
            stream, outgoing = loop_state
            active = tick_index == group_index
            return tick_work(stream, outgoing, layer_now, active, inverse)

        final_stream, last_state = lax.fori_loop(
            0, group_count, one_tick, (final_stream, zero_state)
        )
    return lax.all_to_all(final_stream, "tok", split_axis=0, concat_axis=1, tiled=True)


def solution(mesh):
    in_specs = (
        P(("group", "tok"), None),
        P(None, "group"),
        P(None, None, "tok"),
        P(None, None, "tok", None, None),
        P(None, "tok"),
        P(),
    )
    out_specs = P(("group", "tok"), None)
    return jax.shard_map(body, mesh=mesh, in_specs=in_specs, out_specs=out_specs, check_vma=False)
```

profile of v0, /device:TPU:120, one launch (start us, length us, event | category | flops | bytes accessed | tf_op | source)
XLA Modules:
  0.0 1390.3 jit_solution(5411178419686325323)
XLA Ops:
  3.5 8.5 all-to-all-start
  14.0 35.7 %all-to-all-done = bf16[512,16,128]{2,0,1:T(8,128)(2,1)} async-done(((bf16[512,16,128]{2,0,1:T(8,128)(2,1)}), bf16[512,16,128]{2,0,1:T(8,128)(2,1)}, u32[]{:S(2)}, u32[]{:S(2)}) %all-to-all-start) | async-done | bytes 2097184 | tf_op jit(solution)/shard_map/all_to_all | solution.py:77
  52.5 87.6 %psum.14 = f32[8192]{0:T(1024)S(1)} all-reduce(f32[8192]{0:T(1024)S(1)} %bitcast.261), channel_id=1, replica_groups=mesh['group'=16,'tok'=16] {'tok'}, use_global_device_ids=true, to_apply=%region_1.0 | all-reduce | flops 8192 | bytes 65536 | tf_op jit(solution)/shard_map/psum | solution.py:109
  140.2 663.9 %while.34 = (s32[]{:T(128)}, bf16[8192,128]{1,0:T(8,128)(2,1)}, f32[3,1,128,128]{3,2,0,1:T(8,128)S(1)}, s32[]{:T(128)}, f32[2,5,128]{2,1,0:T(8,128)S(1)}, /*inde...) while((s32[]{:T(128)}, bf16[8192,128]{1,0:T(8,128)(2,1)}, ...), condition=%wide.region_8.9_spmd, body=%wide.region_2.8_spmd.sunk | while | flops 3632480256 | bytes 94034832 | solution.py:117
  164.1 24.6 %collective-permute-done = f32[3,1,128,128]{3,2,0,1:T(8,128)S(1)} collective-permute-done((f32[3,1,128,128]{3,2,0,1:T(8,128)S(1)}, f32[3,1,128,128]{3,2,0,1:T(8,128)S(1)}, u32[]{:S(2)}, u32[]{:S(2)}) %collective-permute-start) | collective-permute-done | bytes 196640 | tf_op jit(solution)/shard_map/while/body/eval_jaxpr/ppermute | solution.py:16
  198.8 8.1 collective-permute-done
  208.2 8.4 collective-permute-done
  217.9 8.4 collective-permute-done
  227.5 9.8 collective-permute-done
  238.7 10.8 collective-permute-done
  250.8 9.7 collective-permute-done
  261.8 9.0 collective-permute-done
  289.7 8.4 collective-permute-done
  299.4 469.8 %collective-permute-done = f32[3,1,128,128]{3,2,0,1:T(8,128)S(1)} collective-permute-done((f32[3,1,128,128]{3,2,0,1:T(8,128)S(1)}, f32[3,1,128,128]{3,2,0,1:T(8,128)S(1)}, u32[]{:S(2)}, u32[]{:S(2)}) %collective-permute-start) | collective-permute-done | bytes 196640 | tf_op jit(solution)/shard_map/while/body/eval_jaxpr/ppermute | solution.py:16
  769.2 34.9 %conditional.4 = ((bf16[8192,128]{1,0:T(8,128)(2,1)}, f32[3,1,128,128]{3,2,0,1:T(8,128)S(1)})) conditional(s32[]{:T(128)} %convert_element_type.267, (bf16[8192,128]{1,0:T(8,128)(2,1)}, f32[3,1,128,128]{3,2,0,1:T(8,128)S(1)}) %tuple.101, (bf16[8192,128]{1,0:T(8,128)(2,1)}, f32[2,5,128]{2,1,0:T(8,128)S(1)}, pred[]{:T(512)}, ...), branch_computations={%region_3.3_spmd, %region_4.7_spmd} | conditional | flops 3632480256 | bytes 93248136 | solution.py:104
  806.8 84.2 %psum.15 = f32[8192]{0:T(1024)S(1)} all-reduce(f32[8192]{0:T(1024)S(1)} %multiply_reduce_fusion.4), channel_id=1, replica_groups=mesh['group'=16,'tok'=16] {'tok'}, use_global_device_ids=true, to_apply=%region_10.11 | all-reduce | flops 8192 | bytes 65536 | tf_op jit(solution)/shard_map/psum | solution.py:109
  891.0 453.8 %while.35 = (s32[]{:T(128)}, bf16[8192,128]{1,0:T(8,128)(2,1)}, f32[3,1,128,128]{3,2,0,1:T(8,128)S(1)}, s32[]{:T(128)}, f32[2,5,128]{2,1,0:T(8,128)S(1)}, /*inde...) while((s32[]{:T(128)}, bf16[8192,128]{1,0:T(8,128)(2,1)}, ...), condition=%wide.region_17.18_spmd, body=%wide.region_11.17_spmd.sunk | while | flops 3632480256 | bytes 94034832 | solution.py:117
  929.3 7.8 collective-permute-done.1
  987.0 9.8 collective-permute-done.1
  998.0 8.6 collective-permute-done.1
  1025.8 8.4 collective-permute-done.1
  1035.4 273.3 %collective-permute-done.1 = f32[3,1,128,128]{3,2,0,1:T(8,128)S(1)} collective-permute-done((f32[3,1,128,128]{3,2,0,1:T(8,128)S(1)}, f32[3,1,128,128]{3,2,0,1:T(8,128)S(1)}, u32[]{:S(2)}, u32[]{:S(2)}) %collective-permute-start.1) | collective-permute-done | bytes 196640 | tf_op jit(solution)/shard_map/while/body/eval_jaxpr/ppermute | solution.py:16
  1308.7 36.1 %conditional.5 = ((bf16[8192,128]{1,0:T(8,128)(2,1)}, f32[3,1,128,128]{3,2,0,1:T(8,128)S(1)})) conditional(s32[]{:T(128)} %convert_element_type.268, (bf16[8192,128]{1,0:T(8,128)(2,1)}, f32[3,1,128,128]{3,2,0,1:T(8,128)S(1)}) %tuple.104, (bf16[8192,128]{1,0:T(8,128)(2,1)}, f32[2,5,128]{2,1,0:T(8,128)S(1)}, pred[]{:T(512)}, ...), branch_computations={%region_12.12_spmd, %region_13.16_spmd} | conditional | flops 3632480256 | bytes 93248136 | solution.py:104
  1344.8 37.3 %all_to_all.38 = bf16[16,512,128]{2,1,0:T(8,128)(2,1)} all-to-all(bf16[16,512,128]{2,1,0:T(8,128)(2,1)} %bitcast.82), channel_id=1, replica_groups=mesh['group'=16,'tok'=16] {'tok'}, dimensions={0} | all-to-all | bytes 4194304 | tf_op jit(solution)/shard_map/all_to_all | solution.py:120
  (172 shorter events, 245.0 us)
Async XLA Ops:
  3.5 46.3 %all-to-all-start = ((bf16[512,16,128]{2,0,1:T(8,128)(2,1)}), bf16[512,16,128]{2,0,1:T(8,128)(2,1)}, u32[]{:S(2)}, u32[]{:S(2)}) async-start(bf16[512,16,128]{2,0,1:T(8,128)(2,1)} %copy_bitcast_fusion), calls=%async_computation | async-start | bytes 4194304 | tf_op jit(solution)/shard_map/all_to_all | solution.py:77
  162.8 25.9 %collective-permute-start = (f32[3,1,128,128]{3,2,0,1:T(8,128)S(1)}, f32[3,1,128,128]{3,2,0,1:T(8,128)S(1)}, u32[]{:S(2)}, u32[]{:S(2)}) collective-permute-start(f32[3,1,128,128]{3,2,0,1:T(8,128)S(1)} %get-tuple-element.889), channel_id=1, source_target_pairs={{0,16},{16,32},{32,48},{48,64},{64,80},{80,96},{96,112},{112,128},... | collective-permute-start | bytes 589832 | tf_op jit(solution)/shard_map/while/body/eval_jaxpr/ppermute | solution.py:16
  188.7 8.8 collective-permute-start
  197.5 9.4 collective-permute-start
  206.9 9.7 collective-permute-start
  216.6 9.7 collective-permute-start
  226.3 11.1 collective-permute-start
  237.4 12.1 collective-permute-start
  249.5 11.0 collective-permute-start
  260.5 10.3 collective-permute-start
  270.8 8.7 collective-permute-start
  279.5 8.9 collective-permute-start
  288.4 9.7 collective-permute-start
  298.1 471.1 %collective-permute-start = (f32[3,1,128,128]{3,2,0,1:T(8,128)S(1)}, f32[3,1,128,128]{3,2,0,1:T(8,128)S(1)}, u32[]{:S(2)}, u32[]{:S(2)}) collective-permute-start(f32[3,1,128,128]{3,2,0,1:T(8,128)S(1)} %get-tuple-element.889), channel_id=1, source_target_pairs={{0,16},{16,32},{32,48},{48,64},{64,80},{80,96},{96,112},{112,128},... | collective-permute-start | bytes 589832 | tf_op jit(solution)/shard_map/while/body/eval_jaxpr/ppermute | solution.py:16
  928.0 9.1 collective-permute-start.1
  937.1 9.1 collective-permute-start.1
  946.2 8.2 collective-permute-start.1
  977.1 8.6 collective-permute-start.1
  985.7 11.1 collective-permute-start.1
  996.8 9.9 collective-permute-start.1
  1006.7 8.7 collective-permute-start.1
  1015.4 9.1 collective-permute-start.1
  1024.5 9.7 collective-permute-start.1
  1034.1 274.6 %collective-permute-start.1 = (f32[3,1,128,128]{3,2,0,1:T(8,128)S(1)}, f32[3,1,128,128]{3,2,0,1:T(8,128)S(1)}, u32[]{:S(2)}, u32[]{:S(2)}) collective-permute-start(f32[3,1,128,128]{3,2,0,1:T(8,128)S(1)} %get-tuple-element.925), channel_id=1, source_target_pairs={{0,16},{16,32},{32,48},{48,64},{64,80},{80,96},{96,112},{112,128},... | collective-permute-start | bytes 589832 | tf_op jit(solution)/shard_map/while/body/eval_jaxpr/ppermute | solution.py:16
  (17 other events, 532.3 us)
where the time goes:
time: 1410 us; the launch traced here: 1390 us
  waiting for transfers between devices  1030 us (73%)
  blocking collectives  209 us (15%)
  matrix products  65.7 us (5%)
  starting transfers between devices  49.5 us (4%)
  local copies, waits for them, and re-layouts  15.9 us (1%)
  loops' own time  15.5 us (1%)
    ppermute x32, waiting for transfers between devices, passed_along(): return lax.ppermute(value, axis, pairs)  991 us
    psum x2, blocking collectives, body(): totals = lax.psum(jnp.sum(widened * widened, axis=1), 'tok')  172 us
    ppermute x32, starting transfers between devices, passed_along(): return lax.ppermute(value, axis, pairs)  41 us
    all_to_all x1, blocking collectives, body(): lax.all_to_all(final_stream, 'tok', split_axis=0, concat_axis=1, tiled=True)  37.3 us
    all_to_all x1, waiting for transfers between devices, body(): lax.all_to_all(tokens, 'tok', split_axis=1, concat_axis=0, tiled=True)  35.7 us
  transfers between devices with their start and end apart: 33, of which 33 were waited for; matrix products, arithmetic and copies ran while one was open for 0% of the time, Pallas kernels for 0%

commit v1 on v0

--- a/solution.py
+++ b/solution.py
@@ -106,7 +106,12 @@
     final_stream = start_stream
     for layer_now in range(layer_count):
         widened = final_stream.astype(jnp.float32)
-        totals = lax.psum(jnp.sum(widened * widened, axis=1), "tok")
+
+        def draw_marks(sheet, axis_name):
+            front = lax.all_gather(sheet, axis_name)
+            return jnp.sum(front, 0)
+
+        totals = draw_marks(jnp.sum(widened * widened, axis=1), "tok")
         inverse = lax.rsqrt(totals / width_all + EPSILON)
 
         def one_tick(tick_index, loop_state):

time: 1410 us -> 1330 us (0.943)
  blocking collectives: 209 us -> 96.1 us
  waiting for transfers between devices: 1030 us -> 1060 us
  loops' own time: 15.5 us -> 29.9 us
    psum x2 -> x0, blocking collectives: 172 us -> none  [body(): totals = lax.psum(jnp.sum(widened * widened, axis=1), 'tok')]
    all_gather x0 -> x2, blocking collectives: none -> 60.1 us  [draw_marks(): front = lax.all_gather(sheet, axis_name)]
    ppermute x32, waiting for transfers between devices: 991 us -> 1020 us  [passed_along(): return lax.ppermute(value, axis, pairs)]
    another operation x2, loops' own time: 14.5 us -> 28.9 us  [body(): lax.fori_loop(0, group_count, one_tick, (final_stream, zero_state))]
where the time goes in v1:
time: 1330 us; the launch traced here: 1320 us
  waiting for transfers between devices  1060 us (80%)
  blocking collectives  96.1 us (7%)
  matrix products  65.7 us (5%)
  starting transfers between devices  49.5 us (4%)
  loops' own time  29.9 us (2%)
  local copies, waits for them, and re-layouts  18.7 us (1%)
    ppermute x32, waiting for transfers between devices, passed_along(): return lax.ppermute(value, axis, pairs)  1020 us
    all_gather x2, blocking collectives, draw_marks(): front = lax.all_gather(sheet, axis_name)  60.1 us
    ppermute x32, starting transfers between devices, passed_along(): return lax.ppermute(value, axis, pairs)  41 us
    all_to_all x1, blocking collectives, body(): lax.all_to_all(final_stream, 'tok', split_axis=0, concat_axis=1, tiled=True)  36.1 us
    all_to_all x1, waiting for transfers between devices, body(): lax.all_to_all(tokens, 'tok', split_axis=1, concat_axis=0, tiled=True)  35.7 us
    another operation x2, loops' own time, body(): lax.fori_loop(0, group_count, one_tick, (final_stream, zero_state))  28.9 us
  transfers between devices with their start and end apart: 33, of which 33 were waited for; matrix products, arithmetic and copies ran while one was open for 0% of the time, Pallas kernels for 0%

profile of v1, /device:TPU:120, one launch (start us, length us, event | category | flops | bytes accessed | tf_op | source)
XLA Modules:
  0.0 1323.4 jit_solution(7694147022761658496)
XLA Ops:
  3.5 8.5 all-to-all-start
  14.0 35.7 %all-to-all-done = bf16[512,16,128]{2,0,1:T(8,128)(2,1)} async-done(((bf16[512,16,128]{2,0,1:T(8,128)(2,1)}), bf16[512,16,128]{2,0,1:T(8,128)(2,1)}, u32[]{:S(2)}, u32[]{:S(2)}) %all-to-all-start) | async-done | bytes 2097184 | tf_op jit(solution)/shard_map/all_to_all | solution.py:77
  52.5 33.4 %all-gather.1 = f32[16,1,8192]{2,1,0:T(1,128)S(1)} all-gather(f32[1,1,8192]{2,1,0:T(1,128)S(1)} %reshape.603), channel_id=1, replica_groups=mesh['group'=16,'tok'=16] {'tok'}, dimensions={0}, use_global_device_ids=true | all-gather | bytes 557056 | tf_op jit(solution)/shard_map/all_gather | solution.py:111
  86.3 695.2 %while.34 = (s32[]{:T(128)}, bf16[8192,128]{1,0:T(8,128)(2,1)}, f32[3,1,128,128]{3,2,0,1:T(8,128)S(1)}, s32[]{:T(128)}, f32[2,5,128]{2,1,0:T(8,128)S(1)}, /*inde...) while((s32[]{:T(128)}, bf16[8192,128]{1,0:T(8,128)(2,1)}, ...), condition=%wide.region_8.9_spmd, body=%wide.region_2.8_spmd.sunk | while | flops 3632480256 | bytes 94034832 | solution.py:122
  126.9 16.8 %collective-permute-done = f32[3,1,128,128]{3,2,0,1:T(8,128)S(1)} collective-permute-done((f32[3,1,128,128]{3,2,0,1:T(8,128)S(1)}, f32[3,1,128,128]{3,2,0,1:T(8,128)S(1)}, u32[]{:S(2)}, u32[]{:S(2)}) %collective-permute-start) | collective-permute-done | bytes 196640 | tf_op jit(solution)/shard_map/while/body/eval_jaxpr/ppermute | solution.py:16
  154.1 8.1 collective-permute-done
  163.4 8.4 collective-permute-done
  173.1 8.9 collective-permute-done
  183.3 10.5 collective-permute-done
  195.1 10.6 collective-permute-done
  206.9 9.3 collective-permute-done
  235.5 8.1 collective-permute-done
  244.9 8.4 collective-permute-done
  254.6 491.2 %collective-permute-done = f32[3,1,128,128]{3,2,0,1:T(8,128)S(1)} collective-permute-done((f32[3,1,128,128]{3,2,0,1:T(8,128)S(1)}, f32[3,1,128,128]{3,2,0,1:T(8,128)S(1)}, u32[]{:S(2)}, u32[]{:S(2)}) %collective-permute-start) | collective-permute-done | bytes 196640 | tf_op jit(solution)/shard_map/while/body/eval_jaxpr/ppermute | solution.py:16
  745.8 35.7 %conditional.4 = ((bf16[8192,128]{1,0:T(8,128)(2,1)}, f32[3,1,128,128]{3,2,0,1:T(8,128)S(1)})) conditional(s32[]{:T(128)} %convert_element_type.267, (bf16[8192,128]{1,0:T(8,128)(2,1)}, f32[3,1,128,128]{3,2,0,1:T(8,128)S(1)}) %tuple.103, (bf16[8192,128]{1,0:T(8,128)(2,1)}, f32[2,5,128]{2,1,0:T(8,128)S(1)}, pred[]{:T(512)}, ...), branch_computations={%region_3.3_spmd, %region_4.7_spmd} | conditional | flops 3632480256 | bytes 93248136 | solution.py:104
  784.2 26.7 %all-gather = f32[131072]{0:T(1024)} all-gather(f32[8192]{0:T(1024)S(1)} %multiply_reduce_fusion.4), channel_id=2, replica_groups=mesh['group'=16,'tok'=16] {'tok'}, dimensions={0}, use_global_device_ids=true | all-gather | bytes 557056 | tf_op jit(solution)/shard_map/all_gather | solution.py:111
  812.2 467.0 %while.35 = (s32[]{:T(128)}, bf16[8192,128]{1,0:T(8,128)(2,1)}, f32[3,1,128,128]{3,2,0,1:T(8,128)S(1)}, s32[]{:T(128)}, f32[2,5,128]{2,1,0:T(8,128)S(1)}, /*inde...) while((s32[]{:T(128)}, bf16[8192,128]{1,0:T(8,128)(2,1)}, ...), condition=%wide.region_17.18_spmd, body=%wide.region_11.17_spmd.sunk | while | flops 3632480256 | bytes 94034832 | solution.py:122
  901.9 8.0 collective-permute-done.1
  911.2 9.3 collective-permute-done.1
  939.8 8.1 collective-permute-done.1
  949.2 8.4 collective-permute-done.1
  958.8 283.5 %collective-permute-done.1 = f32[3,1,128,128]{3,2,0,1:T(8,128)S(1)} collective-permute-done((f32[3,1,128,128]{3,2,0,1:T(8,128)S(1)}, f32[3,1,128,128]{3,2,0,1:T(8,128)S(1)}, u32[]{:S(2)}, u32[]{:S(2)}) %collective-permute-start.1) | collective-permute-done | bytes 196640 | tf_op jit(solution)/shard_map/while/body/eval_jaxpr/ppermute | solution.py:16
  1242.4 36.9 %conditional.5 = ((bf16[8192,128]{1,0:T(8,128)(2,1)}, f32[3,1,128,128]{3,2,0,1:T(8,128)S(1)})) conditional(s32[]{:T(128)} %convert_element_type.268, (bf16[8192,128]{1,0:T(8,128)(2,1)}, f32[3,1,128,128]{3,2,0,1:T(8,128)S(1)}) %tuple.106, (bf16[8192,128]{1,0:T(8,128)(2,1)}, f32[2,5,128]{2,1,0:T(8,128)S(1)}, pred[]{:T(512)}, ...), branch_computations={%region_12.12_spmd, %region_13.16_spmd} | conditional | flops 3632480256 | bytes 93248136 | solution.py:104
  1279.3 36.1 %all_to_all.38 = bf16[16,512,128]{2,1,0:T(8,128)(2,1)} all-to-all(bf16[16,512,128]{2,1,0:T(8,128)(2,1)} %bitcast.82), channel_id=1, replica_groups=mesh['group'=16,'tok'=16] {'tok'}, dimensions={0} | all-to-all | bytes 4194304 | tf_op jit(solution)/shard_map/all_to_all | solution.py:125
  (173 shorter events, 254.0 us)
Async XLA Ops:
  3.5 46.3 %all-to-all-start = ((bf16[512,16,128]{2,0,1:T(8,128)(2,1)}), bf16[512,16,128]{2,0,1:T(8,128)(2,1)}, u32[]{:S(2)}, u32[]{:S(2)}) async-start(bf16[512,16,128]{2,0,1:T(8,128)(2,1)} %copy_bitcast_fusion), calls=%async_computation | async-start | bytes 4194304 | tf_op jit(solution)/shard_map/all_to_all | solution.py:77
  100.8 9.0 collective-permute-start
  125.6 18.1 %collective-permute-start = (f32[3,1,128,128]{3,2,0,1:T(8,128)S(1)}, f32[3,1,128,128]{3,2,0,1:T(8,128)S(1)}, u32[]{:S(2)}, u32[]{:S(2)}) collective-permute-start(f32[3,1,128,128]{3,2,0,1:T(8,128)S(1)} %get-tuple-element.911), channel_id=1, source_target_pairs={{0,16},{16,32},{32,48},{48,64},{64,80},{80,96},{96,112},{112,128},... | collective-permute-start | bytes 589832 | tf_op jit(solution)/shard_map/while/body/eval_jaxpr/ppermute | solution.py:16
  143.7 9.1 collective-permute-start
  152.8 9.4 collective-permute-start
  162.2 9.7 collective-permute-start
  171.8 10.2 collective-permute-start
  182.0 11.7 collective-permute-start
  193.8 11.9 collective-permute-start
  205.6 10.6 collective-permute-start
  225.1 9.1 collective-permute-start
  234.2 9.4 collective-permute-start
  243.6 9.7 collective-permute-start
  253.3 492.5 %collective-permute-start = (f32[3,1,128,128]{3,2,0,1:T(8,128)S(1)}, f32[3,1,128,128]{3,2,0,1:T(8,128)S(1)}, u32[]{:S(2)}, u32[]{:S(2)}) collective-permute-start(f32[3,1,128,128]{3,2,0,1:T(8,128)S(1)} %get-tuple-element.911), channel_id=1, source_target_pairs={{0,16},{16,32},{32,48},{48,64},{64,80},{80,96},{96,112},{112,128},... | collective-permute-start | bytes 589832 | tf_op jit(solution)/shard_map/while/body/eval_jaxpr/ppermute | solution.py:16
  826.2 9.0 collective-permute-start.1
  866.5 9.0 collective-permute-start.1
  875.5 9.2 collective-permute-start.1
  900.6 9.3 collective-permute-start.1
  909.9 10.6 collective-permute-start.1
  920.5 9.0 collective-permute-start.1
  929.5 9.0 collective-permute-start.1
  938.5 9.4 collective-permute-start.1
  947.9 9.7 collective-permute-start.1
  957.6 284.8 %collective-permute-start.1 = (f32[3,1,128,128]{3,2,0,1:T(8,128)S(1)}, f32[3,1,128,128]{3,2,0,1:T(8,128)S(1)}, u32[]{:S(2)}, u32[]{:S(2)}) collective-permute-start(f32[3,1,128,128]{3,2,0,1:T(8,128)S(1)} %get-tuple-element.947), channel_id=1, source_target_pairs={{0,16},{16,32},{32,48},{48,64},{64,80},{80,96},{96,112},{112,128},... | collective-permute-start | bytes 589832 | tf_op jit(solution)/shard_map/while/body/eval_jaxpr/ppermute | solution.py:16
  (16 other events, 293.1 us)
